TPU v7x, 32 devices: a whole 2x2x4 slice. The times are simulated.
32 devices in a mesh: gx: 8 (over y, x, core), gy: 4 (over z).
Axes of the slice: x: 2, y: 2, z: 4, core: 2. Of those that a mesh axis runs over, the one named last changes fastest.
Arguments:
- modes: float32 [3, 64, 8192], P(None, None, ('gx', 'gy')), may hold values from -6 to 6
- weights: float32 [8192], P(('gx', 'gy')), may hold values from 0.25 to 4
Outputs:
- tensor: float32 [64, 64, 64], P('gx', 'gy')
All inputs are finite; a program needn't handle non-finite values.
Results may differ from a plain program's by a relative error of at most 0.00018.
Values sent between devices are 32-bit elements; how exact they have to be, the bound alone decides.
A program may use at most 64 MiB of HBM per device.

v0:
```python
import math

import jax
import jax.numpy as jnp
from jax import lax
from jax.sharding import PartitionSpec as P

CX = 1
CY = 2
NZ = 128


def padded_2(block, sides, width):
    for axis, dim in sides:
        count = lax.axis_size(axis)
        forward = [(i, i + 1) for i in range(count - 1)]
        forward.append((count - 1, 0))
        backward = [(target, source) for source, target in forward]
        low = lax.ppermute(
            lax.slice_in_dim(block, block.shape[dim] - width, None, axis=dim), axis, forward
        )
        high = lax.ppermute(lax.slice_in_dim(block, 0, width, axis=dim), axis, backward)
        block = jnp.concatenate([low, block, high], axis=dim)
    return block


def contribution(field, grads, weighted):
    weighted_field = field * weighted
    result = jnp.zeros((field.shape[1], field.shape[1], field.shape[1]), jnp.float32)
    for comp_a in range(3):
        inner = field[0][:, None, :] * grads[0][comp_a][None, :, :]
        inner = inner + field[1][:, None, :] * grads[1][comp_a][None, :, :]
        inner = inner + field[2][:, None, :] * grads[2][comp_a][None, :, :]
        result = result + jnp.einsum(
            "ic,jkc->ijk", weighted_field[comp_a], inner, precision=lax.Precision.HIGHEST
        )
    return result


def per_device(modes, weights):
    mode_count = modes.shape[1]
    count_x = lax.axis_size("gx")
    count_y = lax.axis_size("gy")
    plane_count = NZ // (count_x * count_y)
    cell_count = CX * CY * NZ
    factor = 1.0 / math.sqrt(CX * count_x * CY * count_y * NZ)
    piece_len = plane_count * CY * CX
    blocks = modes.reshape(3 * mode_count, plane_count, count_y, CY, count_x, CX).transpose(
        4, 2, 0, 1, 3, 5
    )
    weight_blocks = weights.reshape(plane_count, count_y, CY, count_x, CX).transpose(3, 1, 0, 2, 4)
    blocks = blocks.reshape(count_x * count_y, 3 * mode_count, piece_len)
    weight_blocks = weight_blocks.reshape(count_x * count_y, 1, piece_len)
    blocks, weight_blocks = (
        lax.all_to_all(blocks, ("gx", "gy"), split_axis=0, concat_axis=2, tiled=True),
        lax.all_to_all(weight_blocks, ("gx", "gy"), split_axis=0, concat_axis=2, tiled=True),
    )
    grid = blocks.reshape(3, mode_count, NZ, CY, CX).transpose(0, 1, 4, 3, 2)
    weight_grid = weight_blocks.reshape(NZ, CY, CX).transpose(2, 1, 0)
    padded = padded_2(grid, (("gx", 2), ("gy", 3)), 1)
    grad_x = (padded[:, :, 2:, 1:-1] - padded[:, :, :-2, 1:-1]) * 0.5
    grad_y = (padded[:, :, 1:-1, 2:] - padded[:, :, 1:-1, :-2]) * 0.5
    grad_z = (jnp.roll(grid, -1, axis=4) - jnp.roll(grid, 1, axis=4)) * 0.5
    flat = grid.reshape(3, mode_count, cell_count)
    flat_grads = jnp.stack([grad_x, grad_y, grad_z]).reshape(3, 3, mode_count, cell_count)
    flat_weights = weight_grid.reshape(cell_count) * factor
    block_len = 256

    def accumulate(index, total):
        return total + contribution(
            flat, [flat_grads[0], flat_grads[1], flat_grads[2]], flat_weights
        )

    total = lax.fori_loop(
        0,
        cell_count // block_len,
        accumulate,
        jnp.zeros((mode_count, mode_count, mode_count), jnp.float32),
    )
    partial_sum = lax.psum_scatter(total, "gy", scatter_dimension=1, tiled=True)
    return lax.psum_scatter(partial_sum, "gx", scatter_dimension=0, tiled=True)


def solution(mesh):
    return jax.shard_map(
        per_device,
        mesh=mesh,
        in_specs=(P(None, None, ("gx", "gy")), P(("gx", "gy"))),
        out_specs=P("gx", "gy", None),
        check_vma=False,
    )
```

profile of v0, /device:TPU:0, one launch (start us, length us, event | category | flops | bytes accessed | tf_op | source)
XLA Modules:
  0.0 179.6 jit_solution(3705753001075567359)
XLA Ops:
  6.5 0.8 reshape.193
  7.5 0.7 copy.81
  8.2 7.3 %all-to-all-start.1 = ((f32[32,1,8]{2,1,0:T(1,128)}), f32[32,1,8]{2,1,0:T(1,128)S(1)}, u32[]{:S(2)}, u32[]{:S(2)}) async-start(f32[32,1,8]{2,1,0:T(1,128)} %copy.81), calls=%async_computation.1 | async-start | bytes 32768 | tf_op jit(solution)/shard_map/all_to_all | solution.py:56
  15.5 1.2 copy.77
  16.7 0.3 reshape.189
  17.2 0.9 reshape.190
  18.0 4.6 %all-to-all-done.1 = f32[32,1,8]{2,1,0:T(1,128)S(1)} async-done(((f32[32,1,8]{2,1,0:T(1,128)}), f32[32,1,8]{2,1,0:T(1,128)S(1)}, u32[]{:S(2)}, u32[]{:S(2)}) %all-to-all-start.1) | async-done | bytes 1056 | tf_op jit(solution)/shard_map/all_to_all | solution.py:56
  22.7 2.6 %all-to-all-start = ((f32[32,192,8]{1,2,0:T(8,128)}), f32[32,192,8]{1,2,0:T(8,128)S(1)}, u32[]{:S(2)}, u32[]{:S(2)}) async-start(f32[32,192,8]{1,2,0:T(8,128)} %reshape.190), calls=%async_computation | async-start | bytes 524288 | tf_op jit(solution)/shard_map/all_to_all | solution.py:55
  25.5 10.0 %all-to-all-done = f32[32,192,8]{1,2,0:T(8,128)S(1)} async-done(((f32[32,192,8]{1,2,0:T(8,128)}), f32[32,192,8]{1,2,0:T(8,128)S(1)}, u32[]{:S(2)}, u32[]{:S(2)}) %all-to-all-start) | async-done | bytes 196640 | tf_op jit(solution)/shard_map/all_to_all | solution.py:55
  35.5 0.2 reshape.191
  35.7 0.2 copy.87
  35.9 0.9 copy.79
  36.7 1.0 fusion.45
  37.8 0.3 collective-permute-start.1
  38.1 2.3 %collective-permute-start = (f32[3,64,1,2,128]{1,0,3,4,2:T(4,128)S(1)}, f32[3,64,1,2,128]{1,0,3,4,2:T(4,128)S(1)}, u32[]{:S(2)}, u32[]{:S(2)}) collective-permute-start(f32[3,64,1,2,128]{1,0,3,4,2:T(4,128)S(1)} %bitcast.111), channel_id=1, source_target_pairs={{4,0},{8,4},{12,8},{16,12},{20,16},{24,20},{28,24},{0,28},{5,1},{9... | collective-permute-start | bytes 589832 | tf_op jit(solution)/shard_map/ppermute | solution.py:22
  40.4 1.1 slice_bitcast_fusion.8
  41.5 0.8 copy.97
  42.3 0.8 copy.95
  43.1 1.1 reshape.192
  44.2 1.6 copy.83
  45.8 1.6 copy.92
  47.4 1.6 copy.85
  49.0 1.9 %copy.98 = f32[1,3,64,1,2,127]{5,2,4,3,1,0:T(8,128)} copy(f32[1,3,64,1,2,127]{2,1,4,5,3,0:T(4,128)} %get-tuple-element.28) | data formatting | bytes 390144 | tf_op jit(solution)/shard_map/jit(_roll_static)/concatenate | solution.py:63
  50.9 0.9 copy.94
  51.8 1.1 fusion.40
  52.9 0.3 fusion.38
  53.2 0.2 fusion.44
  53.7 0.7 broadcast_multiply_fusion
  54.4 0.7 copy_bitcast_fusion.9
  55.0 0.2 copy.86
  55.2 0.2 copy.88
  55.5 0.7 collective-permute-start.3
  56.3 3.1 %collective-permute-start.2 = (f32[3,64,3,1,128]{4,1,3,2,0:T(8,128)S(1)}, f32[3,64,3,1,128]{4,1,3,2,0:T(8,128)S(1)}, u32[]{:S(2)}, u32[]{:S(2)}) collective-permute-start(f32[3,64,3,1,128]{4,1,3,2,0:T(8,128)S(1)} %get-tuple-element.22), channel_id=1, source_target_pairs={{1,0},{2,1},{3,2},{0,3},{5,4},{6,5},{7,6},{4,7},{9,8},{10,9},{11,1... | collective-permute-start | bytes 884744 | tf_op jit(solution)/shard_map/ppermute | solution.py:22
  59.4 0.2 subtract_multiply_fusion.1
  59.6 0.2 fusion.42
  60.2 0.6 copy_bitcast_fusion.2
  60.9 6.4 %collective-permute-done.3 = f32[3,64,3,1,128]{4,1,3,2,0:T(8,128)S(1)} collective-permute-done((f32[3,64,3,1,128]{4,1,3,2,0:T(8,128)S(1)}, f32[3,64,3,1,128]{4,1,3,2,0:T(8,128)S(1)}, u32[]{:S(2)}, u32[]{:S(2)}) %collective-permute-start.3) | collective-permute-done | bytes 294944 | tf_op jit(solution)/shard_map/ppermute | solution.py:19
  67.3 2.5 %collective-permute-done.2 = f32[3,64,3,1,128]{4,1,3,2,0:T(8,128)S(1)} collective-permute-done((f32[3,64,3,1,128]{4,1,3,2,0:T(8,128)S(1)}, f32[3,64,3,1,128]{4,1,3,2,0:T(8,128)S(1)}, u32[]{:S(2)}, u32[]{:S(2)}) %collective-permute-start.2) | collective-permute-done | bytes 294944 | tf_op jit(solution)/shard_map/ppermute | solution.py:22
  69.8 0.3 copy.112
  70.1 0.3 copy.111
  70.3 0.2 subtract_multiply_fusion
  70.5 0.2 fusion.43
  71.2 6.4 %fusion = f32[64,64,64]{2,0,1:T(8,128)S(1)} fusion(f32[64,256]{1,0:T(8,128)S(1)} %get-tuple-element.41, f32[64,256]{1,0:T(8,128)S(1)} %get-tuple-element.42, f32[64,256]{1,0:T(8,128)S(1)} %copy-done.6, f32[64,256]{1,0:T(8,128)S(1)} %get-tuple-element.44, f32[64,256]{1,0:T(8,128)S(1)} %copy-done.4, f32[64,256]{1,0:T(8,128)S(1)} %copy-done.5, ...), kind=kOutput, calls=%fused_computation | convolution fusion | flops 810549248 | bytes 1507328 | tf_op jit(solution)/shard_map/while/body/eval_jaxpr/ic,jkc->ijk/dot_general | solution.py:34
  77.6 6.4 %fusion.6 = f32[64,64,64]{2,0,1:T(8,128)S(1)} fusion(f32[64,256]{1,0:T(8,128)S(1)} %get-tuple-element.47, f32[64,256]{1,0:T(8,128)S(1)} %get-tuple-element.48, f32[64,256]{1,0:T(8,128)S(1)} %bitcast.132, f32[64,256]{1,0:T(8,128)S(1)} %get-tuple-element.44, f32[64,256]{1,0:T(8,128)S(1)} %copy-done.4, f32[64,256]{1,0:T(8,128)S(1)} %copy-done.5, ...), kind=kOutput, calls=%fused_computation.6 | convolution fusion | flops 810549248 | bytes 1507328 | tf_op jit(solution)/shard_map/while/body/eval_jaxpr/ic,jkc->ijk/dot_general | solution.py:34
  83.9 8.0 %add_add_fusion = f32[64,64,64]{2,0,1:T(8,128)} fusion(f32[64,64,64]{2,0,1:T(8,128)S(1)} %fusion, f32[64,64,64]{2,0,1:T(8,128)S(1)} %fusion.6, f32[64,256]{1,0:T(8,128)S(1)} %get-tuple-element.49, f32[64,256]{1,0:T(8,128)S(1)} %get-tuple-element.44, f32[64,256]{1,0:T(8,128)S(1)} %get-tuple-element.50, f32[64,256]{1,0:T(8,128)S(1)} %copy-done.4, ...), kind=kOutput, calls=%fused_computation.21 | convolution fusion | flops 811073536 | bytes 5701632 | tf_op jit(solution)/shard_map/while/body/eval_jaxpr/ic,jkc->ijk/dot_general | solution.py:34
  92.0 42.9 %reduce-scatter.3.cloned.1.call-done = f32[64,16,64]{2,0,1:T(8,128)} async-done(((f32[64,64,64]{2,0,1:T(8,128)}), f32[64,16,64]{2,0,1:T(8,128)}) %reduce-scatter.3.cloned.1.call-update) | async-done | bytes 262160 | tf_op jit(solution)/shard_map/reduce_scatter | solution.py:80
  134.9 36.4 %reduce-scatter.5.cloned.1.call-done = f32[8,16,64]{2,0,1:T(8,128)} async-done(((f32[64,16,64]{2,0,1:T(8,128)}), f32[8,16,64]{2,0,1:T(8,128)}) %reduce-scatter.5.cloned.1.call-update) | async-done | bytes 32784 | tf_op jit(solution)/shard_map/reduce_scatter | solution.py:81
  171.3 1.5 copy.106
  (46 shorter events, 1.8 us)
Async XLA Ops:
  8.2 14.5 %all-to-all-start.1 = ((f32[32,1,8]{2,1,0:T(1,128)}), f32[32,1,8]{2,1,0:T(1,128)S(1)}, u32[]{:S(2)}, u32[]{:S(2)}) async-start(f32[32,1,8]{2,1,0:T(1,128)} %copy.81), calls=%async_computation.1 | async-start | bytes 32768 | tf_op jit(solution)/shard_map/all_to_all | solution.py:56
  22.7 12.8 %all-to-all-start = ((f32[32,192,8]{1,2,0:T(8,128)}), f32[32,192,8]{1,2,0:T(8,128)S(1)}, u32[]{:S(2)}, u32[]{:S(2)}) async-start(f32[32,192,8]{1,2,0:T(8,128)} %reshape.190), calls=%async_computation | async-start | bytes 524288 | tf_op jit(solution)/shard_map/all_to_all | solution.py:55
  25.2 109.6 %reduce-scatter.3.cloned.1.call-start = ((), (), s32[]{:S(2)}) async-start(), calls=%async_computation.4 | async-start | bytes 2621440 | tf_op jit(solution)/shard_map/reduce_scatter | solution.py:80
  37.8 17.2 %collective-permute-start.1 = (f32[3,64,1,2,128]{1,0,3,4,2:T(4,128)S(1)}, f32[3,64,1,2,128]{1,0,3,4,2:T(4,128)S(1)}, u32[]{:S(2)}, u32[]{:S(2)}) collective-permute-start(f32[3,64,1,2,128]{1,0,3,4,2:T(4,128)S(1)} %bitcast.110), channel_id=1, source_target_pairs={{0,4},{4,8},{8,12},{12,16},{16,20},{20,24},{24,28},{28,0},{1,5},{5... | collective-permute-start | bytes 589832 | tf_op jit(solution)/shard_map/ppermute | solution.py:19
  38.1 17.1 %collective-permute-start = (f32[3,64,1,2,128]{1,0,3,4,2:T(4,128)S(1)}, f32[3,64,1,2,128]{1,0,3,4,2:T(4,128)S(1)}, u32[]{:S(2)}, u32[]{:S(2)}) collective-permute-start(f32[3,64,1,2,128]{1,0,3,4,2:T(4,128)S(1)} %bitcast.111), channel_id=1, source_target_pairs={{4,0},{8,4},{12,8},{16,12},{20,16},{24,20},{28,24},{0,28},{5,1},{9... | collective-permute-start | bytes 589832 | tf_op jit(solution)/shard_map/ppermute | solution.py:22
  51.8 2.6 %copy-start.1 = (f32[1,64,1,2,128]{4,3,1,2,0:T(2,128)S(1)}, f32[1,64,1,2,128]{4,3,1,2,0:T(2,128)}, u32[]{:S(2)}) copy-start(f32[1,64,1,2,128]{4,3,1,2,0:T(2,128)} %copy.83) | copy-start | bytes 196612
  51.8 2.6 %copy-start.2 = (f32[1,64,1,2,128]{4,3,1,2,0:T(2,128)S(1)}, f32[1,64,1,2,128]{4,3,1,2,0:T(2,128)}, u32[]{:S(2)}) copy-start(f32[1,64,1,2,128]{4,3,1,2,0:T(2,128)} %copy.85) | copy-start | bytes 196612
  55.5 4.8 %copy-start = (f32[1,64,1,2,128]{4,3,1,2,0:T(2,128)S(1)}, f32[1,64,1,2,128]{4,3,1,2,0:T(2,128)}, u32[]{:S(2)}) copy-start(f32[1,64,1,2,128]{4,3,1,2,0:T(2,128)} %copy.92) | copy-start | bytes 196612
  55.5 11.7 %collective-permute-start.3 = (f32[3,64,3,1,128]{4,1,3,2,0:T(8,128)S(1)}, f32[3,64,3,1,128]{4,1,3,2,0:T(8,128)S(1)}, u32[]{:S(2)}, u32[]{:S(2)}) collective-permute-start(f32[3,64,3,1,128]{4,1,3,2,0:T(8,128)S(1)} %get-tuple-element.20), channel_id=1, source_target_pairs={{0,1},{1,2},{2,3},{3,0},{4,5},{5,6},{6,7},{7,4},{8,9},{9,10},{10,1... | collective-permute-start | bytes 884744 | tf_op jit(solution)/shard_map/ppermute | solution.py:19
  56.3 13.5 %collective-permute-start.2 = (f32[3,64,3,1,128]{4,1,3,2,0:T(8,128)S(1)}, f32[3,64,3,1,128]{4,1,3,2,0:T(8,128)S(1)}, u32[]{:S(2)}, u32[]{:S(2)}) collective-permute-start(f32[3,64,3,1,128]{4,1,3,2,0:T(8,128)S(1)} %get-tuple-element.22), channel_id=1, source_target_pairs={{1,0},{2,1},{3,2},{0,3},{5,4},{6,5},{7,6},{4,7},{9,8},{10,9},{11,1... | collective-permute-start | bytes 884744 | tf_op jit(solution)/shard_map/ppermute | solution.py:22
  70.0 1.2 copy-start.3
  70.0 1.2 copy-start.4
  70.0 1.2 copy-start.5
  70.0 1.2 copy-start.6
  91.9 79.4 %reduce-scatter.5.cloned.1.call-start = ((), (), s32[]{:S(2)}) async-start(), calls=%async_computation.5 | async-start | bytes 589824 | tf_op jit(solution)/shard_map/reduce_scatter | solution.py:81
Sparse Core Ops, SparseCore 0:
  92.1 42.7 reduce-scatter.2
  138.0 33.3 reduce-scatter.4
where the time goes:
time: 180 us
  waiting for transfers between devices  103 us (57%)
  local copies, waits for them, and re-layouts  23.4 us (13%)
  matrix products  20.7 us (12%)
  starting transfers between devices  16.5 us (9%)
  between operations  13.8 us (8%)
  other arithmetic  2.53 us (1%)
    reduce_scatter x1, waiting for transfers between devices, per_device(): partial_sum = lax.psum_scatter(total, 'gy', scatter_dimension=1, tiled=True)  42.9 us
    reduce_scatter x1, waiting for transfers between devices, per_device(): return lax.psum_scatter(partial_sum, 'gx', scatter_dimension=0, tiled=True)  36.4 us
    dot_general x3, matrix products, contribution(): jnp.einsum('ic,jkc->ijk', weighted_field[comp_a], inner, precision=lax.Pr...  20.7 us
    all_to_all x1, waiting for transfers between devices, per_device(): lax.all_to_all(blocks, ('gx', 'gy'), split_axis=0, concat_axis=2, tiled=T...  9.98 us
    all_to_all x1, starting transfers between devices, per_device(): lax.all_to_all(weight_blocks, ('gx', 'gy'), split_axis=0, concat_axis=2,...  7.33 us
    ppermute x2, waiting for transfers between devices, padded_2(): lax.ppermute(lax.slice_in_dim(block, block.shape[dim] - width, None, axis...  6.38 us
    concatenate x6, local copies, waits for them, and re-layouts, per_device(): grad_z = (jnp.roll(grid, -1, axis=4) - jnp.roll(grid, 1, axis=4)) * 0.5  5.47 us
    ppermute x2, starting transfers between devices, padded_2(): lax.ppermute(lax.slice_in_dim(block, 0, width, axis=dim), axis, backward)  5.44 us
  transfers between devices with their start and end apart: 8, of which 6 were waited for; matrix products, arithmetic and copies ran while one was open for 10% of the time, Pallas kernels for 0%

commit v1 on v0

v1 whole, which is shorter than its diff:
```python
import functools
import math

import jax
import jax.numpy as jnp
from jax import lax
from jax.experimental import pallas as pl
from jax.experimental.pallas import tpu as pltpu
from jax.sharding import PartitionSpec as P

CX = 1
CY = 2
LANES = 128
MESH = pl.DeviceIdType.MESH


def partner_of(gx):
    return gx + 1 - 2 * (gx % 2)


def split(value):
    high = value.astype(jnp.bfloat16)
    low = (value - high.astype(jnp.float32)).astype(jnp.bfloat16)
    return high, low


def kernel(
    nx, ny, modes, width, height, factor,
    x_ref, w_ref, out_ref,
    other_x, other_w, edges, halos, weighted, diffs, field2, high_h, low_h, sums, landed,
    near_send, near_recv, far_send, far_recv,
):
    rows, cells = x_ref.shape
    chips = nx // 2
    devices = nx * ny
    plane = width * height
    pack = max(1, LANES // plane)
    own_i = modes // nx
    own_j = modes // ny
    gx, gy = lax.axis_index("gx"), lax.axis_index("gy")
    core, place = gx % 2, gx // 2
    mate = (partner_of(gx), gy)
    flat = gx * ny + gy

    def beside(step, flat_id):
        other = (flat_id + step + devices) % devices
        return other // ny, other % ny

    def mated(device):
        return partner_of(device[0]), device[1]

    before, after = beside(-1, flat), beside(1, flat)
    mate_flat = mate[0] * ny + gy

    barrier = pltpu.get_barrier_semaphore()
    greeted = [mate, before, after, beside(-1, mate_flat), beside(1, mate_flat)]
    for s in range(chips):
        for t in range(ny):
            if s or t:
                greeted.append((((place + s) % chips) * 2 + core, (gy + t) % ny))
    for device in greeted:
        pl.semaphore_signal(barrier, inc=1, device_id=device, device_id_type=MESH)

    for edge, start in ((0, 0), (1, cells - plane)):
        if pack == 1:
            edges[edge] = x_ref[:, start : start + plane]
        else:
            base = start // LANES * LANES
            tile = x_ref[:, base : base + LANES]
            part = rows // pack
            lane = lax.broadcasted_iota(jnp.int32, (part, LANES), 1)
            packed = jnp.zeros((part, LANES), jnp.float32)
            for p in range(pack):
                shift = (p * plane - (start - base)) % LANES
                piece = tile[p * part : (p + 1) * part]
                piece = pltpu.roll(piece, shift, 1) if shift else piece
                packed = jnp.where(lane // plane == p, piece, packed)
            edges[edge] = packed

    pl.semaphore_wait(barrier, len(greeted))

    def near(index, src, dst, device):
        return pltpu.make_async_remote_copy(
            src_ref=src, dst_ref=dst, send_sem=near_send.at[index], recv_sem=near_recv.at[index],
            device_id=device, device_id_type=MESH,
        )

    copies = [
        near(0, edges.at[1], halos.at[0], after),
        near(1, edges.at[0], halos.at[1], before),
        near(2, edges.at[1], halos.at[2], mated(after)),
        near(3, edges.at[0], halos.at[3], mated(before)),
        near(4, w_ref, other_w, mate),
        near(5, x_ref, other_x, mate),
    ]
    for copy in copies:
        copy.start()

    lane = lax.broadcasted_iota(jnp.int32, (modes, cells), 1)
    at_x, at_y = lane % width, lane // width % height

    def rolled(value, step):
        shift = (-step) % cells
        return pltpu.roll(value, shift, 1) if shift else value

    def plane_of(slot, a):
        if pack == 1:
            tile = halos[slot, a * modes : (a + 1) * modes, :]
        else:
            tiles = []
            part = rows // pack
            narrow = lax.broadcasted_iota(jnp.int32, (8, LANES), 1)
            for r in range(a * modes, (a + 1) * modes, 8):
                p, q = r // part, r % part
                piece = halos[slot, q : q + 8, :]
                full = piece
                for m in range(1, pack):
                    full = jnp.where(narrow // plane == (p + m) % pack, pltpu.roll(piece, m * plane, 1), full)
                tiles.append(full)
            tile = jnp.concatenate(tiles, axis=0)
        return jnp.concatenate([tile] * (cells // tile.shape[1]), axis=1)

    def prepare(which, ref, weight_ref):
        columns = slice(which * cells, (which + 1) * cells)
        weight = weight_ref[...] * factor
        for a in range(3):
            value = ref[a * modes : (a + 1) * modes, :]
            for g in range(nx):
                weighted[g, a, :, columns] = value[g * own_i : (g + 1) * own_i] * weight
            high, low = split(value)
            field2[:modes, a * 2 * cells + which * cells : a * 2 * cells + (which + 1) * cells] = high
            field2[modes:, a * 2 * cells + which * cells : a * 2 * cells + (which + 1) * cells] = low
            up = jnp.where(at_x == width - 1, rolled(value, 1 - width), rolled(value, 1))
            down = jnp.where(at_x == 0, rolled(value, width - 1), rolled(value, -1))
            diffs[a, 0, :, columns] = (up - down) * 0.5
            turn = (height - 1) * width
            up = jnp.where(at_y == height - 1, rolled(value, -turn), rolled(value, width))
            down = jnp.where(at_y == 0, rolled(value, turn), rolled(value, -width))
            diffs[a, 1, :, columns] = (up - down) * 0.5

    def prepare_z(which, ref):
        columns = slice(which * cells, (which + 1) * cells)
        for a in range(3):
            value = ref[a * modes : (a + 1) * modes, :]
            up = jnp.where(lane >= cells - plane, plane_of(2 * which + 1, a), rolled(value, plane))
            down = jnp.where(lane < plane, plane_of(2 * which, a), rolled(value, -plane))
            diffs[a, 2, :, columns] = (up - down) * 0.5

    prepare(0, x_ref, w_ref)
    copies[4].wait_recv()
    copies[5].wait_recv()
    prepare(1, other_x, other_w)
    for copy in copies[:4]:
        copy.wait_recv()
    prepare_z(0, x_ref)
    prepare_z(1, other_x)

    both = 2 * cells
    me = place * ny + gy

    def far(s, t):
        to_place, to_gy = (place + s) % chips, (gy + t) % ny
        index = s * ny + t
        return pltpu.make_async_remote_copy(
            src_ref=sums.at[s, pl.ds(pl.multiple_of(to_gy * own_j, own_j), own_j), :],
            dst_ref=landed.at[me],
            send_sem=far_send.at[index], recv_sem=far_recv.at[me],
            device_id=(to_place * 2 + core, to_gy), device_id_type=MESH,
        )

    def block(s):
        group = (place + s) % chips * 2 + core
        for b in range(3):
            for c in range(0, both, LANES):
                tiles = [diffs[a, b, :, c : c + LANES] for a in range(3)]
                scales = [weighted[group, a, :, c : c + LANES] for a in range(3)]
                for i in range(own_i):
                    value = scales[0][i : i + 1] * tiles[0]
                    for a in (1, 2):
                        value = value + scales[a][i : i + 1] * tiles[a]
                    high, low = split(value)
                    place_of = slice(i * modes, (i + 1) * modes), slice(b * both + c, b * both + c + LANES)
                    high_h[place_of] = high
                    low_h[place_of] = low
        dims = (((1,), (1,)), ((), ()))
        main = lax.dot_general(field2[...], high_h[...], dims, preferred_element_type=jnp.float32)
        rest = lax.dot_general(field2[:modes, :], low_h[...], dims, preferred_element_type=jnp.float32)
        sums[s] = main[:modes] + (main[modes:] + rest)

    def step(index, carry):
        s = chips - 1 - index
        block(s)
        for t in range(ny - 1, 0, -1):
            far(s, t).start()

        @pl.when(s > 0)
        def _():
            far(s, 0).start()

        return carry

    lax.fori_loop(0, chips, step, 0)
    landed[me] = sums[0, pl.ds(pl.multiple_of(gy * own_j, own_j), own_j), :]
    for s in range(chips):
        for t in range(ny):
            if s or t:
                source = (place + s) % chips * ny + (gy + t) % ny
                pltpu.make_async_remote_copy(
                    src_ref=landed.at[source], dst_ref=landed.at[source],
                    send_sem=far_send.at[0], recv_sem=far_recv.at[source],
                    device_id=mate, device_id_type=MESH,
                ).wait_recv()
    total = landed[0]
    for q in range(1, chips * ny):
        total = total + landed[q]
    for i in range(own_i):
        out_ref[i] = total[:, i * modes : (i + 1) * modes]
    for copy in copies:
        copy.wait_send()
    for s in range(chips):
        for t in range(ny):
            if s or t:
                far(s, t).wait_send()


def per_device(modes, weights):
    mode_count, cells = modes.shape[1:]
    nx, ny = lax.axis_size("gx"), lax.axis_size("gy")
    width, height = CX * nx, CY * ny
    plane = width * height
    factor = 1.0 / math.sqrt(cells * nx * ny)
    rows = 3 * mode_count
    own_i, own_j = mode_count // nx, mode_count // ny
    pack = max(1, LANES // plane)
    edge = (rows // pack, plane * pack)
    vmem = pl.BlockSpec(memory_space=pltpu.VMEM)
    chips = nx // 2
    near_count, far_count = 6, chips * ny
    return pl.pallas_call(
        functools.partial(kernel, nx, ny, mode_count, width, height, factor),
        out_shape=jax.ShapeDtypeStruct((own_i, own_j, mode_count), jnp.float32),
        in_specs=[vmem, vmem],
        out_specs=vmem,
        scratch_shapes=[
            pltpu.VMEM((rows, cells), jnp.float32),
            pltpu.VMEM((1, cells), jnp.float32),
            pltpu.VMEM((2, *edge), jnp.float32),
            pltpu.VMEM((4, *edge), jnp.float32),
            pltpu.VMEM((nx, 3, own_i, 2 * cells), jnp.float32),
            pltpu.VMEM((3, 3, mode_count, 2 * cells), jnp.float32),
            pltpu.VMEM((2 * mode_count, 6 * cells), jnp.bfloat16),
            pltpu.VMEM((own_i * mode_count, 6 * cells), jnp.bfloat16),
            pltpu.VMEM((own_i * mode_count, 6 * cells), jnp.bfloat16),
            pltpu.VMEM((chips, mode_count, own_i * mode_count), jnp.float32),
            pltpu.VMEM((chips * ny, own_j, own_i * mode_count), jnp.float32),
            pltpu.SemaphoreType.DMA((near_count,)),
            pltpu.SemaphoreType.DMA((near_count,)),
            pltpu.SemaphoreType.DMA((far_count,)),
            pltpu.SemaphoreType.DMA((far_count,)),
        ],
        compiler_params=pltpu.CompilerParams(collective_id=0, has_side_effects=True),
        name="tensor",
    )(modes.reshape(rows, cells), weights.reshape(1, cells))


def solution(mesh):
    return jax.shard_map(
        per_device,
        mesh=mesh,
        in_specs=(P(None, None, ("gx", "gy")), P(("gx", "gy"))),
        out_specs=P("gx", "gy", None),
        check_vma=False,
    )
```

time: 180 us -> 30.4 us (0.17)
  waiting for transfers between devices: 103 us -> 0 us
  Pallas kernels: 0 us -> 28.7 us
  local copies, waits for them, and re-layouts: 23.4 us -> 1.47 us
  matrix products: 20.7 us -> 0 us
  starting transfers between devices: 16.5 us -> 0 us
  between operations: 13.8 us -> 0.01 us
  other arithmetic: 2.53 us -> 0 us
    reduce_scatter x2 -> x0, waiting for transfers between devices: 79.3 us -> none  [the longest x1 42.9 us: per_device(): partial_sum = lax.psum_scatter(total, 'gy', scatter_dimension=1, tiled=True)]
    pallas_call x0 -> x1, Pallas kernels: none -> 28.7 us  [per_device(): pl.pallas_call(functools.partial(kernel, nx, ny, mode_count, width, heigh...]
    dot_general x3 -> x0, matrix products: 20.7 us -> none  [contribution(): jnp.einsum('ic,jkc->ijk', weighted_field[comp_a], inner, precision=lax.Pr...]
    all_to_all x2 -> x0, waiting for transfers between devices: 14.6 us -> none  [the longest x1 9.98 us: per_device(): lax.all_to_all(blocks, ('gx', 'gy'), split_axis=0, concat_axis=2, tiled=T...]
    all_to_all x2 -> x0, starting transfers between devices: 9.91 us -> none  [the longest x1 7.33 us: per_device(): lax.all_to_all(weight_blocks, ('gx', 'gy'), split_axis=0, concat_axis=2,...]
    ppermute x4 -> x0, waiting for transfers between devices: 8.85 us -> none  [the longest x2 6.38 us: padded_2(): lax.ppermute(lax.slice_in_dim(block, block.shape[dim] - width, None, axis...]
    slice x19 -> x0, local copies, waits for them, and re-layouts: 7.55 us -> none  [the longest x7 3.22 us: contribution(): inner = field[0][:, None, :] * grads[0][comp_a][None, :, :]]
    ppermute x4 -> x0, starting transfers between devices: 6.52 us -> none  [the longest x2 5.44 us: padded_2(): lax.ppermute(lax.slice_in_dim(block, 0, width, axis=dim), axis, backward)]
  transfers between devices with their start and end apart: 8 -> 0, of which waited for: 6 -> 0; matrix products, arithmetic and copies ran while one was open for 10% -> 0% of each run, Pallas kernels for 0% -> 0%
where the time goes in v1:
time: 30.4 us; the launch traced here: 30.2 us
  Pallas kernels  28.7 us (94%)
  local copies, waits for them, and re-layouts  1.47 us (5%)
    pallas_call x1, Pallas kernels, per_device(): pl.pallas_call(functools.partial(kernel, nx, ny, mode_count, width, heigh...  28.7 us
    unnamed x1, local copies, waits for them, and re-layouts  1.47 us

profile of v1, /device:TPU:0, one launch (start us, length us, event | category | flops | bytes accessed | tf_op | source)
XLA Modules:
  0.0 30.2 jit_solution(11715884061574277820)
XLA Ops:
  0.0 28.7 %tensor.1 = f32[8,16,64]{2,1,0:T(8,128)} custom-call(f32[192,256]{1,0:T(8,128)} %bitcast.2, f32[1,256]{1,0:T(1,128)} %bitcast.3), custom_call_target="tpu_custom_call" | custom-call | tf_op jit(solution)/shard_map/tensor/pallas_call | solution.py:239
  28.7 1.5 %copy.4 = f32[8,16,64]{2,1,0:T(8,128)} copy(f32[8,16,64]{2,1,0:T(8,128)} %tensor.1) | data formatting | bytes 65536

commit v2 on v1

v2 whole, which is shorter than its diff:
```python
import functools
import math

import jax
import jax.numpy as jnp
from jax import lax
from jax.experimental import pallas as pl
from jax.experimental.pallas import tpu as pltpu
from jax.sharding import PartitionSpec as P

CX = 1
CY = 2
LANES = 128
MESH = pl.DeviceIdType.MESH


def partner_of(gx):
    return gx + 1 - 2 * (gx % 2)


def split(value):
    high = value.astype(jnp.bfloat16)
    low = (value - high.astype(jnp.float32)).astype(jnp.bfloat16)
    return high, low


def kernel(
    nx, ny, modes, width, height, factor,
    x_ref, w_ref, out_ref,
    other_x, other_w, edges, halos, weighted, diffs, field2, high_h, low_h, sums, landed, line, line_in,
    near_send, near_recv, far_send, far_recv, line_send, line_recv,
):
    rows, cells = x_ref.shape
    chips = nx // 2
    devices = nx * ny
    plane = width * height
    pack = max(1, LANES // plane)
    own_i = modes // nx
    own_j = modes // ny
    gx, gy = lax.axis_index("gx"), lax.axis_index("gy")
    core, place = gx % 2, gx // 2
    mate = (partner_of(gx), gy)
    flat = gx * ny + gy

    def beside(step, flat_id):
        other = (flat_id + step + devices) % devices
        return other // ny, other % ny

    def mated(device):
        return partner_of(device[0]), device[1]

    before, after = beside(-1, flat), beside(1, flat)
    mate_flat = mate[0] * ny + gy

    barrier = pltpu.get_barrier_semaphore()
    greeted = [mate, before, after, beside(-1, mate_flat), beside(1, mate_flat)]
    greeted += [((place + s) % chips * 2 + core, gy) for s in range(1, chips)]
    greeted += [(gx, (gy + t) % ny) for t in range(1, ny)]
    for device in greeted:
        pl.semaphore_signal(barrier, inc=1, device_id=device, device_id_type=MESH)

    for edge, start in ((0, 0), (1, cells - plane)):
        if pack == 1:
            edges[edge] = x_ref[:, start : start + plane]
        else:
            base = start // LANES * LANES
            tile = x_ref[:, base : base + LANES]
            part = rows // pack
            lane = lax.broadcasted_iota(jnp.int32, (part, LANES), 1)
            packed = jnp.zeros((part, LANES), jnp.float32)
            for p in range(pack):
                shift = (p * plane - (start - base)) % LANES
                piece = tile[p * part : (p + 1) * part]
                piece = pltpu.roll(piece, shift, 1) if shift else piece
                packed = jnp.where(lane // plane == p, piece, packed)
            edges[edge] = packed

    lane = lax.broadcasted_iota(jnp.int32, (modes, cells), 1)
    at_x, at_y = lane % width, lane // width % height

    def rolled(value, step):
        shift = (-step) % cells
        return pltpu.roll(value, shift, 1) if shift else value

    def plane_of(slot, a):
        if pack == 1:
            tile = halos[slot, a * modes : (a + 1) * modes, :]
        else:
            tiles = []
            part = rows // pack
            narrow = lax.broadcasted_iota(jnp.int32, (8, LANES), 1)
            for r in range(a * modes, (a + 1) * modes, 8):
                p, q = r // part, r % part
                piece = halos[slot, q : q + 8, :]
                full = piece
                for m in range(1, pack):
                    full = jnp.where(narrow // plane == (p + m) % pack, pltpu.roll(piece, m * plane, 1), full)
                tiles.append(full)
            tile = jnp.concatenate(tiles, axis=0)
        return jnp.concatenate([tile] * (cells // tile.shape[1]), axis=1)

    def prepare(which, ref, weight_ref):
        columns = slice(which * cells, (which + 1) * cells)
        weight = weight_ref[...] * factor
        for a in range(3):
            value = ref[a * modes : (a + 1) * modes, :]
            for g in range(nx):
                weighted[g, a, :, columns] = value[g * own_i : (g + 1) * own_i] * weight
            high, low = split(value)
            stage, half = (which, a) if a < 2 else (2, which)
            field2[stage, :modes, half * cells : (half + 1) * cells] = high
            field2[stage, modes:, half * cells : (half + 1) * cells] = low
            up = jnp.where(at_x == width - 1, rolled(value, 1 - width), rolled(value, 1))
            down = jnp.where(at_x == 0, rolled(value, width - 1), rolled(value, -1))
            diffs[a, 0, :, columns] = (up - down) * 0.5
            turn = (height - 1) * width
            up = jnp.where(at_y == height - 1, rolled(value, -turn), rolled(value, width))
            down = jnp.where(at_y == 0, rolled(value, turn), rolled(value, -width))
            diffs[a, 1, :, columns] = (up - down) * 0.5

    def prepare_z(which, ref):
        columns = slice(which * cells, (which + 1) * cells)
        for a in range(3):
            value = ref[a * modes : (a + 1) * modes, :]
            up = jnp.where(lane >= cells - plane, plane_of(2 * which + 1, a), rolled(value, plane))
            down = jnp.where(lane < plane, plane_of(2 * which, a), rolled(value, -plane))
            diffs[a, 2, :, columns] = (up - down) * 0.5

    dims = (((1,), (1,)), ((), ()))

    def block(s, stage):
        group = (place + s) % chips * 2 + core
        for half in range(2):
            b, which = (half, stage) if stage < 2 else (2, half)
            for c in range(0, cells, LANES):
                near_c = slice(which * cells + c, which * cells + c + LANES)
                tiles = [diffs[a, b, :, near_c] for a in range(3)]
                scales = [weighted[group, a, :, near_c] for a in range(3)]
                for i in range(own_i):
                    value = scales[0][i : i + 1] * tiles[0]
                    for a in (1, 2):
                        value = value + scales[a][i : i + 1] * tiles[a]
                    high, low = split(value)
                    place_of = slice(i * modes, (i + 1) * modes), slice(half * cells + c, half * cells + c + LANES)
                    high_h[place_of] = high
                    low_h[place_of] = low
        main = lax.dot_general(field2[stage], high_h[...], dims, preferred_element_type=jnp.float32)
        rest = lax.dot_general(field2[stage, :modes, :], low_h[...], dims, preferred_element_type=jnp.float32)
        value = main[:modes] + (main[modes:] + rest)
        sums[s] = value if stage == 0 else sums[s] + value

    def rows_of(t):
        return pl.ds(pl.multiple_of((gy + t) % ny * own_j, own_j), own_j)

    def far(s, t):
        return pltpu.make_async_remote_copy(
            src_ref=sums.at[s, rows_of(t), :], dst_ref=landed.at[chips - s, t],
            send_sem=far_send.at[s, t], recv_sem=far_recv.at[chips - s, t],
            device_id=((place + s) % chips * 2 + core, gy), device_id_type=MESH,
        )

    def far_in(s, t):
        return pltpu.make_async_remote_copy(
            src_ref=landed.at[s, t], dst_ref=landed.at[s, t],
            send_sem=far_send.at[s, t], recv_sem=far_recv.at[s, t],
            device_id=mate, device_id_type=MESH,
        )

    def along(t):
        return pltpu.make_async_remote_copy(
            src_ref=line.at[t], dst_ref=line_in.at[ny - t],
            send_sem=line_send.at[t], recv_sem=line_recv.at[ny - t],
            device_id=(gx, (gy + t) % ny), device_id_type=MESH,
        )

    def along_in(t):
        return pltpu.make_async_remote_copy(
            src_ref=line_in.at[t], dst_ref=line_in.at[t],
            send_sem=line_send.at[t], recv_sem=line_recv.at[t],
            device_id=mate, device_id_type=MESH,
        )

    def sweep(stage):
        def body(s, carry):
            block(s, stage)
            return carry

        lax.fori_loop(0, chips, body, 0)

    order = list(range(ny - 1, 0, -1)) + [0]
    prepare(0, x_ref, w_ref)
    sweep(0)
    pl.semaphore_wait(barrier, len(greeted))

    def near(index, src, dst, device):
        return pltpu.make_async_remote_copy(
            src_ref=src, dst_ref=dst, send_sem=near_send.at[index], recv_sem=near_recv.at[index],
            device_id=device, device_id_type=MESH,
        )

    copies = [
        near(0, edges.at[1], halos.at[0], after),
        near(1, edges.at[0], halos.at[1], before),
        near(2, edges.at[1], halos.at[2], mated(after)),
        near(3, edges.at[0], halos.at[3], mated(before)),
        near(4, w_ref, other_w, mate),
        near(5, x_ref, other_x, mate),
    ]
    for copy in copies:
        copy.start()

    copies[4].wait_recv()
    copies[5].wait_recv()
    prepare(1, other_x, other_w)
    sweep(1)
    for copy in copies[:4]:
        copy.wait_recv()
    prepare_z(0, x_ref)
    prepare_z(1, other_x)
    for s in range(chips - 1, 0, -1):
        block(s, 2)
        for t in order:
            far(s, t).start()
    block(0, 2)
    for t in order:
        total = sums[0, rows_of(t), :]
        for s in range(1, chips):
            far_in(s, t).wait_recv()
            total = total + landed[s, t]
        line[t] = total
        if t:
            along(t).start()
    total = line[0]
    for t in range(1, ny):
        along_in(t).wait_recv()
        total = total + line_in[t]
    for i in range(own_i):
        out_ref[i] = total[:, i * modes : (i + 1) * modes]
    for copy in copies:
        copy.wait_send()
    for s in range(1, chips):
        for t in range(ny):
            far(s, t).wait_send()
    for t in range(1, ny):
        along(t).wait_send()


def per_device(modes, weights):
    mode_count, cells = modes.shape[1:]
    nx, ny = lax.axis_size("gx"), lax.axis_size("gy")
    width, height = CX * nx, CY * ny
    plane = width * height
    factor = 1.0 / math.sqrt(cells * nx * ny)
    rows = 3 * mode_count
    own_i, own_j = mode_count // nx, mode_count // ny
    pack = max(1, LANES // plane)
    edge = (rows // pack, plane * pack)
    vmem = pl.BlockSpec(memory_space=pltpu.VMEM)
    chips = nx // 2
    near_count = 6
    return pl.pallas_call(
        functools.partial(kernel, nx, ny, mode_count, width, height, factor),
        out_shape=jax.ShapeDtypeStruct((own_i, own_j, mode_count), jnp.float32),
        in_specs=[vmem, vmem],
        out_specs=vmem,
        scratch_shapes=[
            pltpu.VMEM((rows, cells), jnp.float32),
            pltpu.VMEM((1, cells), jnp.float32),
            pltpu.VMEM((2, *edge), jnp.float32),
            pltpu.VMEM((4, *edge), jnp.float32),
            pltpu.VMEM((nx, 3, own_i, 2 * cells), jnp.float32),
            pltpu.VMEM((3, 3, mode_count, 2 * cells), jnp.float32),
            pltpu.VMEM((3, 2 * mode_count, 2 * cells), jnp.bfloat16),
            pltpu.VMEM((own_i * mode_count, 2 * cells), jnp.bfloat16),
            pltpu.VMEM((own_i * mode_count, 2 * cells), jnp.bfloat16),
            pltpu.VMEM((chips, mode_count, own_i * mode_count), jnp.float32),
            pltpu.VMEM((chips, ny, own_j, own_i * mode_count), jnp.float32),
            pltpu.VMEM((ny, own_j, own_i * mode_count), jnp.float32),
            pltpu.VMEM((ny, own_j, own_i * mode_count), jnp.float32),
            pltpu.SemaphoreType.DMA((near_count,)),
            pltpu.SemaphoreType.DMA((near_count,)),
            pltpu.SemaphoreType.DMA((chips, ny)),
            pltpu.SemaphoreType.DMA((chips, ny)),
            pltpu.SemaphoreType.DMA((ny,)),
            pltpu.SemaphoreType.DMA((ny,)),
        ],
        compiler_params=pltpu.CompilerParams(collective_id=0, has_side_effects=True),
        name="tensor",
    )(modes.reshape(rows, cells), weights.reshape(1, cells))


def solution(mesh):
    return jax.shard_map(
        per_device,
        mesh=mesh,
        in_specs=(P(None, None, ("gx", "gy")), P(("gx", "gy"))),
        out_specs=P("gx", "gy", None),
        check_vma=False,
    )
```

time: 30.4 us -> 28.7 us (0.944)
  Pallas kernels: 28.7 us -> 27.1 us
    pallas_call x1, Pallas kernels: 28.7 us -> 27.1 us  [per_device(): pl.pallas_call(functools.partial(kernel, nx, ny, mode_count, width, heigh...]
where the time goes in v2:
time: 28.7 us; the launch traced here: 28.5 us
  Pallas kernels  27.1 us (94%)
  local copies, waits for them, and re-layouts  1.47 us (5%)
    pallas_call x1, Pallas kernels, per_device(): pl.pallas_call(functools.partial(kernel, nx, ny, mode_count, width, heigh...  27.1 us
    unnamed x1, local copies, waits for them, and re-layouts  1.47 us

profile of v2, /device:TPU:0, one launch (start us, length us, event | category | flops | bytes accessed | tf_op | source)
XLA Modules:
  0.0 28.5 jit_solution(7147060027609001076)
XLA Ops:
  0.0 27.1 %tensor.1 = f32[8,16,64]{2,1,0:T(8,128)} custom-call(f32[192,256]{1,0:T(8,128)} %bitcast.2, f32[1,256]{1,0:T(1,128)} %bitcast.3), custom_call_target="tpu_custom_call" | custom-call | tf_op jit(solution)/shard_map/tensor/pallas_call | solution.py:261
  27.1 1.5 %copy.4 = f32[8,16,64]{2,1,0:T(8,128)} copy(f32[8,16,64]{2,1,0:T(8,128)} %tensor.1) | data formatting | bytes 65536

commit v3 on v2

--- a/solution.py
+++ b/solution.py
@@ -40,21 +40,26 @@
     gx, gy = lax.axis_index("gx"), lax.axis_index("gy")
     core, place = gx % 2, gx // 2
     mate = (partner_of(gx), gy)
+    minor = 2 - chips % 2
+    major = chips // minor
+
+    def shifted(s):
+        return (place // minor + s // minor) % major * minor + (place % minor + s % minor) % minor
+
+    def mirrored(s):
+        return -(s // minor) % major * minor + -(s % minor) % minor
+
     flat = gx * ny + gy
 
     def beside(step, flat_id):
         other = (flat_id + step + devices) % devices
         return other // ny, other % ny
 
-    def mated(device):
-        return partner_of(device[0]), device[1]
-
     before, after = beside(-1, flat), beside(1, flat)
-    mate_flat = mate[0] * ny + gy
 
     barrier = pltpu.get_barrier_semaphore()
-    greeted = [mate, before, after, beside(-1, mate_flat), beside(1, mate_flat)]
-    greeted += [((place + s) % chips * 2 + core, gy) for s in range(1, chips)]
+    greeted = [mate, before, after]
+    greeted += [(shifted(s) * 2 + core, gy) for s in range(1, chips) if s < minor or s % minor == 0]
     greeted += [(gx, (gy + t) % ny) for t in range(1, ny)]
     for device in greeted:
         pl.semaphore_signal(barrier, inc=1, device_id=device, device_id_type=MESH)
@@ -129,7 +134,7 @@
     dims = (((1,), (1,)), ((), ()))
 
     def block(s, stage):
-        group = (place + s) % chips * 2 + core
+        group = shifted(s) * 2 + core
         for half in range(2):
             b, which = (half, stage) if stage < 2 else (2, half)
             for c in range(0, cells, LANES):
@@ -152,11 +157,19 @@
     def rows_of(t):
         return pl.ds(pl.multiple_of((gy + t) % ny * own_j, own_j), own_j)
 
+    def along_minor(s, t):
+        return s % minor > 0 and (s < minor or t % 2 == 0)
+
     def far(s, t):
-        return pltpu.make_async_remote_copy(
-            src_ref=sums.at[s, rows_of(t), :], dst_ref=landed.at[chips - s, t],
-            send_sem=far_send.at[s, t], recv_sem=far_recv.at[chips - s, t],
-            device_id=((place + s) % chips * 2 + core, gy), device_id_type=MESH,
+        if along_minor(s, t):
+            hop, slot = s % minor, s
+        else:
+            hop = s // minor * minor
+            slot = mirrored(hop) + s % minor
+        return pltpu.make_async_remote_copy(
+            src_ref=sums.at[s, rows_of(t), :], dst_ref=landed.at[slot, t],
+            send_sem=far_send.at[s, t], recv_sem=far_recv.at[slot, t],
+            device_id=(shifted(hop) * 2 + core, gy), device_id_type=MESH,
         )
 
     def far_in(s, t):
@@ -201,30 +214,54 @@
     copies = [
         near(0, edges.at[1], halos.at[0], after),
         near(1, edges.at[0], halos.at[1], before),
-        near(2, edges.at[1], halos.at[2], mated(after)),
-        near(3, edges.at[0], halos.at[3], mated(before)),
+        near(2, halos.at[0], halos.at[2], mate),
+        near(3, halos.at[1], halos.at[3], mate),
         near(4, w_ref, other_w, mate),
         near(5, x_ref, other_x, mate),
     ]
-    for copy in copies:
-        copy.start()
+    for index in (0, 1, 4, 5):
+        copies[index].start()
 
     copies[4].wait_recv()
     copies[5].wait_recv()
     prepare(1, other_x, other_w)
     sweep(1)
-    for copy in copies[:4]:
-        copy.wait_recv()
+    for index in (0, 1):
+        copies[index].wait_recv()
+        copies[index + 2].start()
     prepare_z(0, x_ref)
+    for index in (2, 3):
+        copies[index].wait_recv()
     prepare_z(1, other_x)
-    for s in range(chips - 1, 0, -1):
+    cross = [s for s in range(chips) if s % minor and s >= minor]
+    inner = list(range(1, minor))
+    outer = [s for s in range(minor, chips, minor)]
+
+    def waits_for(s, t):
+        if minor == 1:
+            return []
+        if t % 2 == 0:
+            return [s + 1] if s in outer else []
+        return cross if s in inner else []
+
+    for s in cross + inner + outer:
         block(s, 2)
         for t in order:
-            far(s, t).start()
+            if not waits_for(s, t):
+                far(s, t).start()
     block(0, 2)
     for t in order:
+        for s in inner + outer:
+            if waits_for(s, t):
+                value = sums[s, rows_of(t), :]
+                for source in waits_for(s, t):
+                    far_in(source, t).wait_recv()
+                    value = value + landed[source, t]
+                sums[s, rows_of(t), :] = value
+                far(s, t).start()
+    for t in order:
         total = sums[0, rows_of(t), :]
-        for s in range(1, chips):
+        for s in inner + outer:
             far_in(s, t).wait_recv()
             total = total + landed[s, t]
         line[t] = total

time: 28.7 us -> 27.3 us (0.951)
  Pallas kernels: 27.1 us -> 25.6 us
    pallas_call x1, Pallas kernels: 27.1 us -> 25.6 us  [per_device(): pl.pallas_call(functools.partial(kernel, nx, ny, mode_count, width, heigh...]
where the time goes in v3:
time: 27.3 us; the launch traced here: 27.1 us
  Pallas kernels  25.6 us (94%)
  local copies, waits for them, and re-layouts  1.47 us (5%)
    pallas_call x1, Pallas kernels, per_device(): pl.pallas_call(functools.partial(kernel, nx, ny, mode_count, width, heigh...  25.6 us
    unnamed x1, local copies, waits for them, and re-layouts  1.47 us

profile of v3, /device:TPU:0, one launch (start us, length us, event | category | flops | bytes accessed | tf_op | source)
XLA Modules:
  0.0 27.1 jit_solution(2682614202957021208)
XLA Ops:
  0.0 25.6 %tensor.1 = f32[8,16,64]{2,1,0:T(8,128)} custom-call(f32[192,256]{1,0:T(8,128)} %bitcast.2, f32[1,256]{1,0:T(1,128)} %bitcast.3), custom_call_target="tpu_custom_call" | custom-call | tf_op jit(solution)/shard_map/tensor/pallas_call | solution.py:298
  25.6 1.5 %copy.4 = f32[8,16,64]{2,1,0:T(8,128)} copy(f32[8,16,64]{2,1,0:T(8,128)} %tensor.1) | data formatting | bytes 65536
